TPU v7x, 256 devices: a whole 4x4x8 slice. The times are simulated.
256 devices in a mesh: row: 16 (over z_hi, y), col: 16 (over x, z_lo, core).
Axes of the slice: x: 4, y: 4, z: 8 (z_hi: 4, z_lo: 2; z = z_hi * 2 + z_lo), core: 2. Of those that a mesh axis runs over, the one named last changes fastest.
Arguments:
- positions: float32 [3, 32768], P(None, ('row', 'col')), may hold values from 0 to 1
- radii: float32 [32768], P(('row', 'col')), may hold values from 0.5 to 2
- right_side: float32 [32768, 256], P(('row', 'col')), may hold values from -60 to 60, as said below
Outputs:
- solution: float32 [32768, 256], P(('row', 'col'))
- residual: float32 [32768, 256], P(('row', 'col'))
Inputs may be any that keep to these rules, and one draw needn't show every extreme that they name: `right_side`: real values of varying scale.
All inputs are finite; a program needn't handle non-finite values.
Results may differ from a plain program's by a relative error of at most 0.0003.
Values sent between devices are 32-bit elements; how exact they have to be, the bound alone decides.
A program may use at most 64 MiB of HBM per device.

v0:
```python
import jax
import jax.numpy as jnp
from jax import lax
from jax.sharding import PartitionSpec as P

ITERS = 2


def kernel_product(row_points, col_points, values, kernel_scale, softening, limit):
    row_count = row_points.shape[1]
    col_count = col_points.shape[1]
    blocks = max(1, row_count * col_count // limit)
    while row_count % blocks:
        blocks = blocks - 1
    block_size = row_count // blocks
    grouped = row_points.reshape(3, blocks, block_size).transpose(1, 0, 2)

    def apply_block(row_block):
        first = row_block[0][:, None] - col_points[0][None, :]
        second = row_block[1][:, None] - col_points[1][None, :]
        third = row_block[2][:, None] - col_points[2][None, :]
        squared = first * first + second * second + third * third
        weights = lax.rsqrt(squared + softening) * kernel_scale
        return jnp.dot(
            weights, values, preferred_element_type=jnp.float32, precision=lax.Precision.HIGHEST
        )

    return lax.map(apply_block, grouped).reshape(row_count, values.shape[1])


def constants(total):
    kernel_scale = float(total) ** (-0.5)
    spacing = 0.25 * float(total) ** (-1.0 / 3.0)
    return (kernel_scale, spacing * spacing)


def squares(residual):
    return lax.psum(jnp.sum(residual * residual, axis=0), ("row", "col"))


def body(positions, radii, right_side):
    local_count = positions.shape[1]
    total = local_count * lax.axis_size("row") * lax.axis_size("col")
    kernel_scale, softening = constants(total)
    row_points = lax.all_gather(positions, "col", axis=1, tiled=True)
    col_points = lax.all_gather(positions, "row", axis=1, tiled=True)
    limit = 1 << 20
    solution = jnp.zeros_like(right_side)
    residual = right_side
    direction = right_side
    norm_now = squares(residual)
    for iteration in range(ITERS):
        col_values = lax.all_gather(direction, "row", axis=0, tiled=True)
        summed = lax.psum_scatter(
            kernel_product(row_points, col_points, col_values, kernel_scale, softening, limit),
            "col",
            scatter_dimension=0,
            tiled=True,
        )
        image_vec = direction / radii[:, None] + summed
        curvature = lax.psum(jnp.sum(direction * image_vec, axis=0), ("row", "col"))
        step_size = norm_now / curvature
        solution = solution + step_size * direction
        residual = residual - step_size * image_vec
        if iteration + 1 < ITERS:
            norm_next = squares(residual)
            direction = residual + norm_next / norm_now * direction
            norm_now = norm_next
    return (solution, residual)


def solution(mesh):
    return jax.shard_map(
        body,
        mesh=mesh,
        in_specs=(P(None, ("row", "col")), P(("row", "col")), P(("row", "col"), None)),
        out_specs=(P(("row", "col"), None), P(("row", "col"), None)),
        check_vma=False,
    )
```

profile of v0, /device:TPU:1, one launch (start us, length us, event | category | flops | bytes accessed | tf_op | source)
XLA Modules:
  0.0 550.6 jit_solution(2993443880854321543)
XLA Ops:
  7.2 0.0 all-gather.3.cloned.1.call-start
  7.2 0.7 all-gather.3.cloned.1.call-update
  7.9 0.0 reduce-scatter.3.cloned.1.call-start
  7.9 40.7 %all_gather.13 = f32[3,2048]{1,0:T(4,128)S(1)} all-gather(f32[3,128]{1,0:T(4,128)} %param.7), channel_id=1, replica_groups=mesh['row'=16,'col'=16] {'row'}, dimensions={1}, use_global_device_ids=true | all-gather | bytes 26112 | tf_op jit(solution)/shard_map/all_gather | solution.py:46
  48.7 28.0 %all_gather.12 = f32[3,2048]{1,0:T(4,128)S(1)} all-gather(f32[3,128]{1,0:T(4,128)} %param.7), channel_id=1, replica_groups=mesh['row'=16,'col'=16] {'col'}, dimensions={1}, use_global_device_ids=true | all-gather | bytes 26112 | tf_op jit(solution)/shard_map/all_gather | solution.py:45
  76.6 0.0 all-gather.3.cloned.1.call-done
  76.6 0.2 broadcast.19.clone
  76.8 25.9 %while.20 = (s32[]{:T(128)}, f32[4,512,256]{2,1,0:T(8,128)S(1)}, f32[4,3,512]{2,1,0:T(4,128)S(1)}, f32[3,2048]{1,0:T(4,128)S(1)}, f32[2048,256]{1,0:T(8,128)}, /*index=5*/s32[]{:T(128)}, s32[]{:T(128)}, s32[]{}, s32[]{}) while((s32[]{:T(128)}, f32[4,512,256]{2,1,0:T(8,128)S(1)}, f32[4,3,512]{2,1,0:T(4,128)S(1)}, f32[3,2048]{1,0:T(4,128)S(1)}, ...), condition=%wide.region_3.4_spmd, body=%wide.region_2.3_spmd.sunk | while | flops 3231711232 | bytes 2713733 | solution.py:28
  76.8 6.4 %fusion.71 = f32[4,512,256]{2,1,0:T(8,128)S(1)} fusion(f32[4,512,256]{2,1,0:T(8,128)S(1)} %get-tuple-element.194, s32[]{:T(128)} %get-tuple-element.193, f32[2048,256]{1,0:T(8,128)} %get-tuple-element.206, f32[2048]{0:T(1024)S(1)} %bitcast.63, f32[512]{0:T(512)S(1)} %bitcast.70, f32[2048]{0:T(1024)S(1)} %bitcast.64, f32[512]{0:T(512)S(1)} %bitcast.69, ...), kind=kOutput, calls=%fused_computation.21.clone.1 | convolution fusion | flops 3231711232 | bytes 2652164 | tf_op jit(solution)/shard_map/while/body/eval_jaxpr/dot_general | solution.py:24
  83.3 6.4 %fusion.71 = f32[4,512,256]{2,1,0:T(8,128)S(1)} fusion(f32[4,512,256]{2,1,0:T(8,128)S(1)} %get-tuple-element.194, s32[]{:T(128)} %get-tuple-element.193, f32[2048,256]{1,0:T(8,128)} %get-tuple-element.206, f32[2048]{0:T(1024)S(1)} %bitcast.63, f32[512]{0:T(512)S(1)} %bitcast.70, f32[2048]{0:T(1024)S(1)} %bitcast.64, f32[512]{0:T(512)S(1)} %bitcast.69, ...), kind=kOutput, calls=%fused_computation.21.clone.1 | convolution fusion | flops 3231711232 | bytes 2652164 | tf_op jit(solution)/shard_map/while/body/eval_jaxpr/dot_general | solution.py:24
  89.8 6.4 %fusion.71 = f32[4,512,256]{2,1,0:T(8,128)S(1)} fusion(f32[4,512,256]{2,1,0:T(8,128)S(1)} %get-tuple-element.194, s32[]{:T(128)} %get-tuple-element.193, f32[2048,256]{1,0:T(8,128)} %get-tuple-element.206, f32[2048]{0:T(1024)S(1)} %bitcast.63, f32[512]{0:T(512)S(1)} %bitcast.70, f32[2048]{0:T(1024)S(1)} %bitcast.64, f32[512]{0:T(512)S(1)} %bitcast.69, ...), kind=kOutput, calls=%fused_computation.21.clone.1 | convolution fusion | flops 3231711232 | bytes 2652164 | tf_op jit(solution)/shard_map/while/body/eval_jaxpr/dot_general | solution.py:24
  96.3 6.4 %fusion.71 = f32[4,512,256]{2,1,0:T(8,128)S(1)} fusion(f32[4,512,256]{2,1,0:T(8,128)S(1)} %get-tuple-element.194, s32[]{:T(128)} %get-tuple-element.193, f32[2048,256]{1,0:T(8,128)} %get-tuple-element.206, f32[2048]{0:T(1024)S(1)} %bitcast.63, f32[512]{0:T(512)S(1)} %bitcast.70, f32[2048]{0:T(1024)S(1)} %bitcast.64, f32[512]{0:T(512)S(1)} %bitcast.69, ...), kind=kOutput, calls=%fused_computation.21.clone.1 | convolution fusion | flops 3231711232 | bytes 2652164 | tf_op jit(solution)/shard_map/while/body/eval_jaxpr/dot_general | solution.py:24
  102.7 0.0 copy-start.1
  102.7 0.0 copy-start.2
  102.7 0.0 copy-start.4
  102.7 1.3 copy-done.1
  104.0 0.0 reduce-scatter.3.cloned.1.call-update
  104.1 0.0 all-gather.5.cloned.1.call-start
  104.1 58.5 %reduce-scatter.3.cloned.1.call-done = f32[128,256]{1,0:T(8,128)} async-done(((f32[2048,256]{1,0:T(8,128)}), f32[128,256]{1,0:T(8,128)}) %reduce-scatter.3.cloned.1.call-update) | async-done | bytes 131088 | tf_op jit(solution)/shard_map/reduce_scatter | solution.py:54
  162.6 0.0 copy-done.2
  162.6 0.0 copy-done.4
  162.6 1.0 multiply_reduce_fusion.2
  163.6 79.5 %all-reduce = (f32[256]{0:T(256)S(1)}, f32[256]{0:T(256)S(1)}) all-reduce(f32[256]{0:T(256)S(1)} %get-tuple-element.59, f32[256]{0:T(256)S(1)} %get-tuple-element.58), channel_id=1, replica_groups=mesh['row'=16,'col'=16] {'row','col'}, use_global_device_ids=true, to_apply=%region_1.0 | all-reduce | flops 512 | bytes 4096 | tf_op jit(solution)/shard_map/psum | solution.py:38
  243.1 1.0 multiply_reduce_fusion.1
  244.1 72.5 %psum.30 = f32[256]{0:T(256)S(1)} all-reduce(f32[256]{0:T(256)S(1)} %get-tuple-element.82), channel_id=1, replica_groups=mesh['row'=16,'col'=16] {'row','col'}, use_global_device_ids=true, to_apply=%region_8.9 | all-reduce | flops 256 | bytes 2048 | tf_op jit(solution)/shard_map/psum | solution.py:38
  316.6 0.7 multiply_add_fusion.1
  317.3 0.0 all-gather.5.cloned.1.call-update
  317.3 0.2 reduce-scatter.5.cloned.1.call-start
  317.6 55.1 %all-gather.5.cloned.1.call-done = f32[2048,256]{1,0:T(8,128)} async-done(((f32[128,256]{1,0:T(8,128)}), f32[2048,256]{1,0:T(8,128)}) %all-gather.5.cloned.1.call-update) | async-done | bytes 2097168 | tf_op jit(solution)/shard_map/all_gather | solution.py:53
  372.7 0.2 broadcast.19
  372.9 25.9 %while.21 = (s32[]{:T(128)}, f32[4,512,256]{2,1,0:T(8,128)S(1)}, f32[4,3,512]{2,1,0:T(4,128)S(1)}, f32[3,2048]{1,0:T(4,128)S(1)}, f32[2048,256]{1,0:T(8,128)}, /*index=5*/s32[]{:T(128)}, s32[]{:T(128)}, s32[]{}, s32[]{}) while((s32[]{:T(128)}, f32[4,512,256]{2,1,0:T(8,128)S(1)}, f32[4,3,512]{2,1,0:T(4,128)S(1)}, f32[3,2048]{1,0:T(4,128)S(1)}, ...), condition=%wide.region_10.11_spmd, body=%wide.region_9.10_spmd.sunk | while | flops 3231711232 | bytes 2713733 | solution.py:28
  372.9 6.4 %fusion.75 = f32[4,512,256]{2,1,0:T(8,128)S(1)} fusion(f32[4,512,256]{2,1,0:T(8,128)S(1)} %get-tuple-element.221, s32[]{:T(128)} %get-tuple-element.220, f32[2048,256]{1,0:T(8,128)} %get-tuple-element.233, f32[2048]{0:T(1024)S(1)} %bitcast.66, f32[512]{0:T(512)S(1)} %bitcast.73, f32[2048]{0:T(1024)S(1)} %bitcast.67, f32[512]{0:T(512)S(1)} %bitcast.72, ...), kind=kOutput, calls=%fused_computation.48.clone.1 | convolution fusion | flops 3231711232 | bytes 2652164 | tf_op jit(solution)/shard_map/while/body/eval_jaxpr/dot_general | solution.py:24
  379.4 6.4 %fusion.75 = f32[4,512,256]{2,1,0:T(8,128)S(1)} fusion(f32[4,512,256]{2,1,0:T(8,128)S(1)} %get-tuple-element.221, s32[]{:T(128)} %get-tuple-element.220, f32[2048,256]{1,0:T(8,128)} %get-tuple-element.233, f32[2048]{0:T(1024)S(1)} %bitcast.66, f32[512]{0:T(512)S(1)} %bitcast.73, f32[2048]{0:T(1024)S(1)} %bitcast.67, f32[512]{0:T(512)S(1)} %bitcast.72, ...), kind=kOutput, calls=%fused_computation.48.clone.1 | convolution fusion | flops 3231711232 | bytes 2652164 | tf_op jit(solution)/shard_map/while/body/eval_jaxpr/dot_general | solution.py:24
  385.9 6.4 %fusion.75 = f32[4,512,256]{2,1,0:T(8,128)S(1)} fusion(f32[4,512,256]{2,1,0:T(8,128)S(1)} %get-tuple-element.221, s32[]{:T(128)} %get-tuple-element.220, f32[2048,256]{1,0:T(8,128)} %get-tuple-element.233, f32[2048]{0:T(1024)S(1)} %bitcast.66, f32[512]{0:T(512)S(1)} %bitcast.73, f32[2048]{0:T(1024)S(1)} %bitcast.67, f32[512]{0:T(512)S(1)} %bitcast.72, ...), kind=kOutput, calls=%fused_computation.48.clone.1 | convolution fusion | flops 3231711232 | bytes 2652164 | tf_op jit(solution)/shard_map/while/body/eval_jaxpr/dot_general | solution.py:24
  392.3 6.4 %fusion.75 = f32[4,512,256]{2,1,0:T(8,128)S(1)} fusion(f32[4,512,256]{2,1,0:T(8,128)S(1)} %get-tuple-element.221, s32[]{:T(128)} %get-tuple-element.220, f32[2048,256]{1,0:T(8,128)} %get-tuple-element.233, f32[2048]{0:T(1024)S(1)} %bitcast.66, f32[512]{0:T(512)S(1)} %bitcast.73, f32[2048]{0:T(1024)S(1)} %bitcast.67, f32[512]{0:T(512)S(1)} %bitcast.72, ...), kind=kOutput, calls=%fused_computation.48.clone.1 | convolution fusion | flops 3231711232 | bytes 2652164 | tf_op jit(solution)/shard_map/while/body/eval_jaxpr/dot_general | solution.py:24
  398.7 0.0 copy-start
  398.7 0.0 copy-start.3
  398.8 1.3 copy-done
  400.1 0.0 reduce-scatter.5.cloned.1.call-update
  400.1 61.9 %reduce-scatter.5.cloned.1.call-done = f32[128,256]{1,0:T(8,128)} async-done(((f32[2048,256]{1,0:T(8,128)}), f32[128,256]{1,0:T(8,128)}) %reduce-scatter.5.cloned.1.call-update) | async-done | bytes 131088 | tf_op jit(solution)/shard_map/reduce_scatter | solution.py:54
  462.0 0.0 copy-done.3
  462.0 1.0 multiply_reduce_fusion
  463.0 79.4 %psum.31 = f32[256]{0:T(256)S(1)} all-reduce(f32[256]{0:T(256)S(1)} %multiply_reduce_fusion), channel_id=1, replica_groups=mesh['row'=16,'col'=16] {'row','col'}, use_global_device_ids=true, to_apply=%region_13.14 | all-reduce | flops 256 | bytes 2048 | tf_op jit(solution)/shard_map/psum | solution.py:61
  542.4 1.7 multiply_subtract_fusion
  (19 shorter events, 0.3 us)
Async XLA Ops:
  7.2 69.5 %all-gather.3.cloned.1.call-start = ((), (), s32[]{:S(2)}) async-start(), calls=%async_computation.2 | async-start | bytes 2228224 | tf_op jit(solution)/shard_map/all_gather | solution.py:53
  7.9 154.7 %reduce-scatter.3.cloned.1.call-start = ((), (), s32[]{:S(2)}) async-start(), calls=%async_computation.3 | async-start | bytes 2228224 | tf_op jit(solution)/shard_map/reduce_scatter | solution.py:54
  102.7 1.3 copy-start.1
  102.7 59.9 %copy-start.2 = (f32[128,256]{1,0:T(8,128)S(1)}, f32[128,256]{1,0:T(8,128)}, u32[]{:S(2)}) copy-start(f32[128,256]{1,0:T(8,128)} %param.9) | copy-start | bytes 393220
  102.7 59.9 %copy-start.4 = (f32[128]{0:T(128)S(1)}, f32[128]{0:T(128)}, u32[]{:S(2)}) copy-start(f32[128]{0:T(128)} %param.8) | copy-start | bytes 1540
  104.1 268.6 %all-gather.5.cloned.1.call-start = ((), (), s32[]{:S(2)}) async-start(), calls=%async_computation.4 | async-start | bytes 2228224 | tf_op jit(solution)/shard_map/all_gather | solution.py:53
  317.3 144.7 %reduce-scatter.5.cloned.1.call-start = ((), (), s32[]{:S(2)}) async-start(), calls=%async_computation.5 | async-start | bytes 2228224 | tf_op jit(solution)/shard_map/reduce_scatter | solution.py:54
  398.7 1.3 copy-start
  398.7 63.2 %copy-start.3 = (f32[128,256]{1,0:T(8,128)S(1)}, f32[128,256]{1,0:T(8,128)}, u32[]{:S(2)}) copy-start(f32[128,256]{1,0:T(8,128)} %multiply_add_fusion.1) | copy-start | bytes 393220
Sparse Core Ops, SparseCore 0:
  10.4 62.6 all-gather.2
  104.2 58.3 reduce-scatter.2
  317.4 55.2 all-gather.4
  400.2 61.7 reduce-scatter.4
where the time goes:
time: 551 us
  blocking collectives  300 us (54%)
  waiting for transfers between devices  176 us (32%)
  matrix products  51.2 us (9%)
  between operations  13.8 us (3%)
    psum x2, blocking collectives, squares(): return lax.psum(jnp.sum(residual * residual, axis=0), ('row', 'col'))  152 us
    reduce_scatter x2, waiting for transfers between devices, body(): lax.psum_scatter(kernel_product(row_points, col_points, col_values, kerne...  120 us
    psum x1, blocking collectives, body(): curvature = lax.psum(jnp.sum(direction * image_vec, axis=0), ('row', 'col'))  79.4 us
    all_gather x2, waiting for transfers between devices, body(): col_values = lax.all_gather(direction, 'row', axis=0, tiled=True)  55.1 us
    dot_general x8, matrix products, apply_block(): jnp.dot(weights, values, preferred_element_type=jnp.float32, precision=la...  51.2 us
    all_gather x1, blocking collectives, body(): col_points = lax.all_gather(positions, 'row', axis=1, tiled=True)  40.7 us
    all_gather x1, blocking collectives, body(): row_points = lax.all_gather(positions, 'col', axis=1, tiled=True)  28 us
  transfers between devices with their start and end apart: 4, of which 3 were waited for; matrix products, arithmetic and copies ran while one was open for 0% of the time, Pallas kernels for 0%

commit v1 on v0

v1 whole, which is shorter than its diff:
```python
import functools

import jax
import jax.numpy as jnp
from jax import lax
from jax.experimental import pallas as pl
from jax.experimental.pallas import tpu as pltpu
from jax.sharding import PartitionSpec as P

MESH = pl.DeviceIdType.MESH
B = 128
R = 256
NX, NY, NZ = 4, 4, 8
PLANE = NX * NY
LINE = NZ * 2
HALF = B // 2
SUB = 4
SR = B // SUB
F32 = jnp.float32
BF16 = jnp.bfloat16


def constants(total):
    kernel_scale = float(total) ** (-0.5)
    spacing = 0.25 * float(total) ** (-1.0 / 3.0)
    return (kernel_scale, spacing * spacing)


def kernel(
    kernel_scale, softening,
    pos_ref, rad_ref, b_ref, sol_ref, res_ref,
    khi, klo, gath, vhi, vlo, part, sib, ring, xb, ppos, lpos, own_pos, w1, w2, r1, ar_src, ar_plane, ar_line,
    pos_send, pos_recv, g_send, g_recv, s_send, s_recv, r_send, r_recv, ar_send, ar_recv,
):
    row, col = lax.axis_index("row"), lax.axis_index("col")
    x, y = col // 4, lax.rem(row, 4)
    z, k = (row // 4) * 2 + lax.rem(col // 2, 2), lax.rem(col, 2)

    def device(xx, yy, zz, kk):
        return {"row": (zz // 2) * 4 + yy, "col": xx * 4 + lax.rem(zz, 2) * 2 + kk}

    def at_x(d):
        return lax.rem(x + d, NX)

    def at_y(d):
        return lax.rem(y + d, NY)

    def at_z(d):
        return lax.rem(z + d, NZ)

    def send(src, dst, ssem, rsem, dev):
        pltpu.make_async_remote_copy(
            src_ref=src, dst_ref=dst, send_sem=ssem, recv_sem=rsem, device_id=dev, device_id_type=MESH
        ).start()

    def wait(ref, sem):
        pltpu.make_async_copy(ref, ref, sem).wait()

    plane_peers = [device(at_x(dx), at_y(dy), z, k) for dx in range(NX) for dy in range(NY) if dx or dy]
    line_peers = [
        device(x, y, at_z(dz), lax.rem(k + dk, 2)) for dz in range(NZ) for dk in range(2) if dz or dk
    ]
    sibling = device(x, y, z, 1 - k)
    slot = x * NY + y
    line_slot = z * 2 + k

    barrier = pltpu.get_barrier_semaphore()
    for peer in plane_peers + line_peers:
        pl.semaphore_signal(barrier, 1, device_id=peer, device_id_type=MESH)
    own_pos[...] = jnp.zeros_like(own_pos)
    own_pos[0:3, :] = pos_ref[...]
    own_pos[3:4, :] = rad_ref[...]
    pl.semaphore_wait(barrier, len(plane_peers) + len(line_peers))

    def half_rows(h):
        return pl.ds(h * HALF, HALF)

    def gather_start(m, src, h):
        for d in (2, 1, 3):
            first = device(at_x(d), y, z, k) if h == 0 else device(x, at_y(d), z, k)
            send(src.at[half_rows(h)], gath.at[m, slot, half_rows(h)], g_send.at[m], g_recv.at[m, h, slot], first)
        for d in (2, 1, 3):
            second = device(x, at_y(d), z, k) if h == 0 else device(at_x(d), y, z, k)
            send(src.at[half_rows(h)], gath.at[m, slot, half_rows(h)], g_send.at[m], g_recv.at[m, h, slot], second)

    def gather_forward(m):
        for o in (1, 3, 2):
            for h in range(2):
                s = at_x(o) * NY + y if h == 0 else x * NY + at_y(o)
                piece = gath.at[m, s, half_rows(h)]
                wait(piece, g_recv.at[m, h, s])
                for d in (2, 1, 3):
                    second = device(x, at_y(d), z, k) if h == 0 else device(at_x(d), y, z, k)
                    send(piece, piece, g_send.at[m], g_recv.at[m, h, s], second)

    def gather_finish(m):
        for dx in range(NX):
            for dy in range(NY):
                s = at_x(dx) * NY + at_y(dy)
                for h in range(2):
                    if (dy if h == 0 else dx) != 0:
                        wait(gath.at[m, s, half_rows(h)], g_recv.at[m, h, s])

    def sum_start(i):
        ar_plane[i, slot] = ar_src[i]
        for peer in plane_peers:
            send(ar_src.at[i], ar_plane.at[i, slot], ar_send.at[i, 0], ar_recv.at[i, 0], peer)

    def sum_middle(i):
        wait(ar_plane.at[i, 0 : PLANE - 1], ar_send.at[i, 0])
        wait(ar_plane.at[i, 0 : PLANE - 1], ar_recv.at[i, 0])
        total = ar_plane[i, 0]
        for s in range(1, PLANE):
            total = total + ar_plane[i, s]
        ar_src[i] = total
        ar_line[i, line_slot] = total
        for peer in line_peers:
            send(ar_src.at[i], ar_line.at[i, line_slot], ar_send.at[i, 1], ar_recv.at[i, 1], peer)

    def sum_finish(i):
        wait(ar_line.at[i, 0 : LINE - 1], ar_recv.at[i, 1])
        total = ar_line[i, 0]
        for s in range(1, LINE):
            total = total + ar_line[i, s]
        return total

    for peer in plane_peers:
        send(own_pos, ppos.at[slot], pos_send, pos_recv.at[0], peer)
    for peer in line_peers:
        send(own_pos, lpos.at[line_slot], pos_send, pos_recv.at[1], peer)
    gather_start(0, b_ref, 0)
    gather_start(0, b_ref, 1)
    ppos[slot] = own_pos[...]
    lpos[line_slot] = own_pos[...]
    gath[0, slot] = b_ref[...]
    inverse_radii = 1.0 / own_pos[...].T[:, 3:4]

    wait(ppos.at[0 : PLANE - 1], pos_recv.at[0])
    wait(lpos.at[0 : LINE - 1], pos_recv.at[1])
    gather_forward(0)

    def spread(t, _):
        rows = pl.ds(pl.multiple_of(t * B, B), B)
        turned = lpos[t].T
        for c in range(3):
            xb[c, rows, :] = jnp.broadcast_to(turned[:, c : c + 1], (B, B))
        return 0

    lax.fori_loop(0, LINE, spread, 0)

    def evaluate(t, _):
        rows = pl.ds(pl.multiple_of(t * B, B), B)
        for j in range(PLANE):
            d0 = xb[0, rows, :] - ppos[j, 0:1, :]
            d1 = xb[1, rows, :] - ppos[j, 1:2, :]
            d2 = xb[2, rows, :] - ppos[j, 2:3, :]
            weight = lax.rsqrt(d0 * d0 + d1 * d1 + d2 * d2 + softening)
            high = weight.astype(BF16)
            khi[rows, j * B : (j + 1) * B] = high
            klo[rows, j * B : (j + 1) * B] = (weight - high.astype(F32)).astype(BF16)
        return 0

    lax.fori_loop(0, LINE, evaluate, 0)

    def split_values(m):
        def step(s, _):
            rows = pl.ds(pl.multiple_of(s * B, B), B)
            value = gath[m, s]
            high = value.astype(BF16)
            vhi[rows, :] = high
            vlo[rows, :] = (value - high.astype(F32)).astype(BF16)
            return 0

        lax.fori_loop(0, PLANE, step, 0)

    def sub_rows(c):
        return pl.ds(c * SR, SR)

    def ring_target(way, s):
        return at_z(4 - s) if way == 0 else at_z(4 + s)

    def ring_peer(way):
        return device(x, y, at_z(1 if way == 0 else NZ - 1), k)

    def join_sibling(m, dest):
        wait(sib.at[m, dest], s_recv.at[m, dest])
        mine = pl.ds(pl.multiple_of(dest * 2 * B + k * B, B), B)
        sib[m, dest] = sib[m, dest] + part[mine, :]

    def ring_step(m, s):
        if s == 0:
            for c in range(SUB // 2):
                for way in range(2):
                    cc = c if way == 0 else c + SUB // 2
                    piece = sib.at[m, ring_target(way, 0), sub_rows(cc)]
                    send(piece, ring.at[m, way, 0, sub_rows(cc)], r_send.at[m], r_recv.at[m, way, 0, cc], ring_peer(way))
            return
        late = ((0, 1), (2, 3))
        for i in range(SUB):
            for way in range(2):
                order = late[1 - way] + late[way]
                c = order[i]
                dest = ring_target(way, s)
                if s == 1 and c not in late[way]:
                    piece = sib.at[m, dest, sub_rows(c)]
                else:
                    piece = ring.at[m, way, s - 1, sub_rows(c)]
                    wait(piece, r_recv.at[m, way, s - 1, c])
                    piece[...] = piece[...] + sib[m, dest, sub_rows(c), :]
                send(piece, ring.at[m, way, s, sub_rows(c)], r_send.at[m], r_recv.at[m, way, s, c], ring_peer(way))

    def ring_result(m, c):
        for way in range(2):
            wait(ring.at[m, way, 3, sub_rows(c)], r_recv.at[m, way, 3, c])
        return sib[m, z, sub_rows(c), :] + ring[m, 0, 3, sub_rows(c), :] + ring[m, 1, 3, sub_rows(c), :]

    def products(m):
        def step(i, _):
            off = 4 + (1 - 2 * lax.rem(i, 2)) * ((i + 1) // 2)
            dest = at_z(off)
            rows = pl.ds(pl.multiple_of(dest * 2 * B, 2 * B), 2 * B)
            high = khi[rows, :]
            total = jnp.dot(klo[rows, :], vhi[...], preferred_element_type=F32)
            total = total + jnp.dot(high, vlo[...], preferred_element_type=F32)
            part[rows, :] = total + jnp.dot(high, vhi[...], preferred_element_type=F32)
            other = pl.ds(pl.multiple_of(dest * 2 * B + (1 - k) * B, B), B)
            send(part.at[other], sib.at[m, dest], s_send.at[m], s_recv.at[m, dest], sibling)

            @pl.when(i == 2)
            def _():
                join_sibling(m, at_z(4))
                ring_step(m, 0)

            return 0

        lax.fori_loop(0, NZ, step, 0)
        for d in (3, 5):
            join_sibling(m, at_z(d))
        ring_step(m, 1)
        for d in (2, 6, 1, 7, 0):
            join_sibling(m, at_z(d))

    gather_finish(0)
    split_values(0)
    products(0)
    ring_step(0, 2)
    ring_step(0, 3)
    for h in range(2):
        for c in range(h * SUB // 2, (h + 1) * SUB // 2):
            rows = slice(c * SR, (c + 1) * SR)
            w1[rows, :] = b_ref[rows, :] * inverse_radii[rows] + kernel_scale * ring_result(0, c)
        gather_start(1, w1, h)
    gath[1, slot] = w1[...]
    b = b_ref[...]
    ar_src[0] = jnp.zeros((8, R), F32)
    ar_src[0, 0:1, :] = jnp.sum(b * b, axis=0, keepdims=True)
    ar_src[0, 1:2, :] = jnp.sum(b * w1[...], axis=0, keepdims=True)
    sum_start(0)
    wait(gath.at[0, 0:NZ], s_send.at[0])
    gather_forward(1)
    sum_middle(0)
    gather_finish(1)
    split_values(1)
    sums = sum_finish(0)
    norm0 = sums[0:1, :]
    alpha = norm0 / sums[1:2, :]
    r1[...] = b_ref[...] - alpha * w1[...]
    ar_src[1] = jnp.zeros((8, R), F32)
    ar_src[1, 0:1, :] = jnp.sum(r1[...] * r1[...], axis=0, keepdims=True)
    sum_start(1)
    products(1)
    sum_middle(1)
    ring_step(1, 2)
    ring_step(1, 3)
    norm1 = sum_finish(1)[0:1, :]
    beta = norm1 / norm0
    for c in range(SUB):
        rows = slice(c * SR, (c + 1) * SR)
        w2[rows, :] = w1[rows, :] * inverse_radii[rows] + kernel_scale * ring_result(1, c)
    direction = r1[...] + beta * b_ref[...]
    w2[...] = (1.0 + beta) * w1[...] - alpha * w2[...]
    ar_src[2] = jnp.zeros((8, R), F32)
    ar_src[2, 0:1, :] = jnp.sum(direction * w2[...], axis=0, keepdims=True)
    sum_start(2)
    sum_middle(2)
    step_size = norm1 / sum_finish(2)[0:1, :]
    sol_ref[...] = alpha * b_ref[...] + step_size * (r1[...] + beta * b_ref[...])
    res_ref[...] = r1[...] - step_size * w2[...]

    wait(ar_plane.at[0, 0 : PLANE - 1], pos_send)
    for m in range(2):
        wait(gath.at[m, 0 : PLANE - 1], g_send.at[m])
        wait(gath.at[m, 0 : NZ - 1], r_send.at[m])
    wait(gath.at[1, 0:NZ], s_send.at[1])
    for i in range(3):
        wait(ar_line.at[i, 0 : LINE - 1], ar_send.at[i, 1])


def body(positions, radii, right_side):
    total = B * lax.axis_size("row") * lax.axis_size("col")
    kernel_scale, softening = constants(total)
    vmem = pl.BlockSpec(memory_space=pltpu.VMEM)
    out = jax.ShapeDtypeStruct((B, R), F32)
    dma = pltpu.SemaphoreType.DMA
    cols = PLANE * B
    return pl.pallas_call(
        functools.partial(kernel, kernel_scale, softening),
        out_shape=(out, out),
        in_specs=[vmem] * 3,
        out_specs=(vmem, vmem),
        scratch_shapes=[
            pltpu.VMEM((LINE * B, cols), BF16),
            pltpu.VMEM((LINE * B, cols), BF16),
            pltpu.VMEM((2, PLANE, B, R), F32),
            pltpu.VMEM((cols, R), BF16),
            pltpu.VMEM((cols, R), BF16),
            pltpu.VMEM((LINE * B, R), F32),
            pltpu.VMEM((2, NZ, B, R), F32),
            pltpu.VMEM((2, 2, 4, B, R), F32),
            pltpu.VMEM((3, LINE * B, B), F32),
            pltpu.VMEM((PLANE, 8, B), F32),
            pltpu.VMEM((LINE, 8, B), F32),
            pltpu.VMEM((8, B), F32),
            pltpu.VMEM((B, R), F32),
            pltpu.VMEM((B, R), F32),
            pltpu.VMEM((B, R), F32),
            pltpu.VMEM((3, 8, R), F32),
            pltpu.VMEM((3, PLANE, 8, R), F32),
            pltpu.VMEM((3, LINE, 8, R), F32),
            dma,
            dma((2,)),
            dma((2,)),
            dma((2, 2, PLANE)),
            dma((2,)),
            dma((2, NZ)),
            dma((2,)),
            dma((2, 2, 4, SUB)),
            dma((3, 2)),
            dma((3, 2)),
        ],
        compiler_params=pltpu.CompilerParams(
            collective_id=0, has_side_effects=True, vmem_limit_bytes=56 << 20
        ),
        name="cg",
    )(positions, radii.reshape(1, B), right_side)


def solution(mesh):
    return jax.shard_map(
        body,
        mesh=mesh,
        in_specs=(P(None, ("row", "col")), P(("row", "col")), P(("row", "col"), None)),
        out_specs=(P(("row", "col"), None), P(("row", "col"), None)),
        check_vma=False,
    )
```

time: 551 us -> 109 us (0.20)
  blocking collectives: 300 us -> 0 us
  waiting for transfers between devices: 176 us -> 0 us
  Pallas kernels: 0 us -> 106 us
  matrix products: 51.2 us -> 0 us
  between operations: 13.8 us -> 0.65 us
    psum x3 -> x0, blocking collectives: 231 us -> none  [the longest x2 152 us: squares(): return lax.psum(jnp.sum(residual * residual, axis=0), ('row', 'col'))]
    reduce_scatter x2 -> x0, waiting for transfers between devices: 120 us -> none  [body(): lax.psum_scatter(kernel_product(row_points, col_points, col_values, kerne...]
    pallas_call x0 -> x1, Pallas kernels: none -> 106 us  [body(): pl.pallas_call(functools.partial(kernel, kernel_scale, softening), out_sh...]
    all_gather x2 -> x0, blocking collectives: 68.7 us -> none  [the longest x1 40.7 us: body(): col_points = lax.all_gather(positions, 'row', axis=1, tiled=True)]
    all_gather x2 -> x0, waiting for transfers between devices: 55.1 us -> none  [body(): col_values = lax.all_gather(direction, 'row', axis=0, tiled=True)]
    dot_general x8 -> x0, matrix products: 51.2 us -> none  [apply_block(): jnp.dot(weights, values, preferred_element_type=jnp.float32, precision=la...]
  transfers between devices with their start and end apart: 4 -> 0, of which waited for: 3 -> 0; matrix products, arithmetic and copies ran while one was open for 0% -> 0% of each run, Pallas kernels for 0% -> 0%
where the time goes in v1:
time: 109 us
  Pallas kernels  106 us (97%)
  local copies, waits for them, and re-layouts  2.26 us (2%)
    pallas_call x1, Pallas kernels, body(): pl.pallas_call(functools.partial(kernel, kernel_scale, softening), out_sh...  106 us
    unnamed x4, local copies, waits for them, and re-layouts  2.26 us

profile of v1, /device:TPU:1, one launch (start us, length us, event | category | flops | bytes accessed | tf_op | source)
XLA Modules:
  0.0 109.0 jit_solution(9755453584041208868)
XLA Ops:
  0.6 106.1 %cg.1 = (f32[128,256]{1,0:T(8,128)}, f32[128,256]{1,0:T(8,128)}) custom-call(f32[3,128]{1,0:T(4,128)} %pos_ref.1, f32[1,128]{1,0:T(1,128)} %bitcast.1, f32[128,256]{1,0:T(8,128)} %b_ref.1), custom_call_target="tpu_custom_call" | custom-call | tf_op jit(solution)/shard_map/cg/pallas_call | solution.py:306
  106.7 0.0 copy-start
  106.8 1.6 %copy.7 = f32[128,256]{1,0:T(8,128)} copy(f32[128,256]{1,0:T(8,128)} %get-tuple-element.4) | data formatting | bytes 262144
  108.4 0.0 copy-done
  108.4 0.7 copy.8
Async XLA Ops:
  106.7 1.6 %copy-start = (f32[128,256]{1,0:T(8,128)S(1)}, f32[128,256]{1,0:T(8,128)}, u32[]{:S(2)}) copy-start(f32[128,256]{1,0:T(8,128)} %get-tuple-element.5) | copy-start | bytes 393220

commit v2 on v1

--- a/solution.py
+++ b/solution.py
@@ -29,8 +29,8 @@
 def kernel(
     kernel_scale, softening,
     pos_ref, rad_ref, b_ref, sol_ref, res_ref,
-    khi, klo, gath, vhi, vlo, part, sib, ring, xb, ppos, lpos, own_pos, w1, w2, r1, ar_src, ar_plane, ar_line,
-    pos_send, pos_recv, g_send, g_recv, s_send, s_recv, r_send, r_recv, ar_send, ar_recv,
+    khi, klo, gath, vhi, vlo, part, sib, ring, xb, ppos, lpos, own_pos, inv, w1, ar_src, ar_plane, ar_line,
+    pos_send, pos_recv, g_send, g_recv, q_recv, s_send, s_recv, r_send, r_recv, ar_send, ar_recv,
 ):
     row, col = lax.axis_index("row"), lax.axis_index("col")
     x, y = col // 4, lax.rem(row, 4)
@@ -75,31 +75,58 @@
     def half_rows(h):
         return pl.ds(h * HALF, HALF)
 
+    def plane_slot(h, first, second):
+        return at_x(first) * NY + at_y(second) if h == 0 else at_x(second) * NY + at_y(first)
+
+    def first_peer(h, d):
+        return device(at_x(d), y, z, k) if h == 0 else device(x, at_y(d), z, k)
+
+    def second_peer(h, d):
+        return device(x, at_y(d), z, k) if h == 0 else device(at_x(d), y, z, k)
+
+    def first_at(h, d):
+        return at_x(d) if h == 0 else at_y(d)
+
     def gather_start(m, src, h):
         for d in (2, 1, 3):
-            first = device(at_x(d), y, z, k) if h == 0 else device(x, at_y(d), z, k)
-            send(src.at[half_rows(h)], gath.at[m, slot, half_rows(h)], g_send.at[m], g_recv.at[m, h, slot], first)
-        for d in (2, 1, 3):
-            second = device(x, at_y(d), z, k) if h == 0 else device(at_x(d), y, z, k)
-            send(src.at[half_rows(h)], gath.at[m, slot, half_rows(h)], g_send.at[m], g_recv.at[m, h, slot], second)
-
-    def gather_forward(m):
+            send(src.at[half_rows(h)], gath.at[m, slot, half_rows(h)], g_send.at[m], g_recv.at[m, h, slot], first_peer(h, d))
+        for d in (1, 3):
+            send(src.at[half_rows(h)], gath.at[m, slot, half_rows(h)], g_send.at[m], g_recv.at[m, h, slot], second_peer(h, d))
+
+    def gather_spread(m):
         for o in (1, 3, 2):
             for h in range(2):
-                s = at_x(o) * NY + y if h == 0 else x * NY + at_y(o)
+                s = plane_slot(h, o, 0)
                 piece = gath.at[m, s, half_rows(h)]
                 wait(piece, g_recv.at[m, h, s])
-                for d in (2, 1, 3):
-                    second = device(x, at_y(d), z, k) if h == 0 else device(at_x(d), y, z, k)
-                    send(piece, piece, g_send.at[m], g_recv.at[m, h, s], second)
+                for d in (1, 3):
+                    send(piece, piece, g_send.at[m], g_recv.at[m, h, s], second_peer(h, d))
+
+    def quarter(m, h, s, q):
+        return gath.at[m, s, pl.ds(h * HALF + q * HALF // 2, HALF // 2)]
+
+    def gather_forward(m, offsets):
+        for o in offsets:
+            for h in range(2):
+                for q in range(2):
+                    s = plane_slot(h, o, 3 if q == 0 else 1)
+                    wait(gath.at[m, s, half_rows(h)], g_recv.at[m, h, s])
+                    piece = quarter(m, h, s, q)
+                    send(piece, piece, g_send.at[m], q_recv.at[m, h, q, first_at(h, o)], second_peer(h, 1 if q == 0 else 3))
 
     def gather_finish(m):
-        for dx in range(NX):
-            for dy in range(NY):
-                s = at_x(dx) * NY + at_y(dy)
-                for h in range(2):
-                    if (dy if h == 0 else dx) != 0:
-                        wait(gath.at[m, s, half_rows(h)], g_recv.at[m, h, s])
+        for o in (0, 1, 3, 2):
+            for h in range(2):
+                for q in range(2):
+                    wait(quarter(m, h, plane_slot(h, o, 2), q), q_recv.at[m, h, q, first_at(h, o)])
+
+    def pack(i, j, term):
+        column = jnp.sum(term, axis=0, keepdims=True)
+        ar_src[i, 2 * j : 2 * j + 1, :] = column[:, :B]
+        ar_src[i, 2 * j + 1 : 2 * j + 2, :] = column[:, B:]
+
+    def unpack(total, j):
+        return jnp.concatenate([total[2 * j : 2 * j + 1, :], total[2 * j + 1 : 2 * j + 2, :]], axis=1)
 
     def sum_start(i):
         ar_plane[i, slot] = ar_src[i]
@@ -124,29 +151,29 @@
             total = total + ar_line[i, s]
         return total
 
+    for peer in line_peers:
+        send(own_pos, lpos.at[line_slot], pos_send, pos_recv.at[1], peer)
     for peer in plane_peers:
         send(own_pos, ppos.at[slot], pos_send, pos_recv.at[0], peer)
-    for peer in line_peers:
-        send(own_pos, lpos.at[line_slot], pos_send, pos_recv.at[1], peer)
     gather_start(0, b_ref, 0)
     gather_start(0, b_ref, 1)
     ppos[slot] = own_pos[...]
     lpos[line_slot] = own_pos[...]
     gath[0, slot] = b_ref[...]
-    inverse_radii = 1.0 / own_pos[...].T[:, 3:4]
-
+    inv[...] = jnp.broadcast_to(1.0 / own_pos[3:4, :], (B, B)).T
+    gather_spread(0)
+    wait(lpos.at[0 : LINE - 1], pos_recv.at[1])
+
+    def spread(t, _):
+        for u in range(4):
+            rows = pl.ds(pl.multiple_of(t * 4 * B + u * B, B), B)
+            for a in range(3):
+                xb[a, rows, :] = jnp.broadcast_to(lpos[t * 4 + u, a : a + 1, :], (B, B)).T
+        return 0
+
+    lax.fori_loop(0, LINE // 4, spread, 0)
+    gather_forward(0, (0,))
     wait(ppos.at[0 : PLANE - 1], pos_recv.at[0])
-    wait(lpos.at[0 : LINE - 1], pos_recv.at[1])
-    gather_forward(0)
-
-    def spread(t, _):
-        rows = pl.ds(pl.multiple_of(t * B, B), B)
-        turned = lpos[t].T
-        for c in range(3):
-            xb[c, rows, :] = jnp.broadcast_to(turned[:, c : c + 1], (B, B))
-        return 0
-
-    lax.fori_loop(0, LINE, spread, 0)
 
     def evaluate(t, _):
         rows = pl.ds(pl.multiple_of(t * B, B), B)
@@ -160,7 +187,11 @@
             klo[rows, j * B : (j + 1) * B] = (weight - high.astype(F32)).astype(BF16)
         return 0
 
-    lax.fori_loop(0, LINE, evaluate, 0)
+    lax.fori_loop(0, 6, evaluate, 0)
+    gather_forward(0, (1, 3))
+    lax.fori_loop(6, 12, evaluate, 0)
+    gather_forward(0, (2,))
+    lax.fori_loop(12, LINE, evaluate, 0)
 
     def split_values(m):
         def step(s, _):
@@ -226,73 +257,85 @@
             other = pl.ds(pl.multiple_of(dest * 2 * B + (1 - k) * B, B), B)
             send(part.at[other], sib.at[m, dest], s_send.at[m], s_recv.at[m, dest], sibling)
 
-            @pl.when(i == 2)
-            def _():
-                join_sibling(m, at_z(4))
-                ring_step(m, 0)
+            for at, work in hooks:
+                pl.when(i == at)(work)
 
             return 0
 
+        def first():
+            join_sibling(m, at_z(4))
+            ring_step(m, 0)
+
+        def second():
+            join_sibling(m, at_z(3))
+            join_sibling(m, at_z(5))
+            ring_step(m, 1)
+
+        hooks = ((1, first), (4, second))
         lax.fori_loop(0, NZ, step, 0)
-        for d in (3, 5):
+        for d in (2, 6):
             join_sibling(m, at_z(d))
-        ring_step(m, 1)
-        for d in (2, 6, 1, 7, 0):
+        ring_step(m, 2)
+        for d in (1, 7):
             join_sibling(m, at_z(d))
-
+        ring_step(m, 3)
+        join_sibling(m, z)
+
+    ar_src[...] = jnp.zeros_like(ar_src)
     gather_finish(0)
     split_values(0)
     products(0)
-    ring_step(0, 2)
-    ring_step(0, 3)
+    pack(0, 0, b_ref[...] * b_ref[...])
     for h in range(2):
         for c in range(h * SUB // 2, (h + 1) * SUB // 2):
             rows = slice(c * SR, (c + 1) * SR)
-            w1[rows, :] = b_ref[rows, :] * inverse_radii[rows] + kernel_scale * ring_result(0, c)
+            own = jnp.concatenate([inv[rows, :], inv[rows, :]], axis=1) * b_ref[rows, :]
+            w1[rows, :] = own + kernel_scale * ring_result(0, c)
         gather_start(1, w1, h)
     gath[1, slot] = w1[...]
-    b = b_ref[...]
-    ar_src[0] = jnp.zeros((8, R), F32)
-    ar_src[0, 0:1, :] = jnp.sum(b * b, axis=0, keepdims=True)
-    ar_src[0, 1:2, :] = jnp.sum(b * w1[...], axis=0, keepdims=True)
+    pack(0, 1, b_ref[...] * w1[...])
     sum_start(0)
     wait(gath.at[0, 0:NZ], s_send.at[0])
-    gather_forward(1)
+    gather_spread(1)
+    gather_forward(1, (0, 1, 3))
     sum_middle(0)
+    gather_forward(1, (2,))
     gather_finish(1)
     split_values(1)
+    products(1)
     sums = sum_finish(0)
-    norm0 = sums[0:1, :]
-    alpha = norm0 / sums[1:2, :]
-    r1[...] = b_ref[...] - alpha * w1[...]
-    ar_src[1] = jnp.zeros((8, R), F32)
-    ar_src[1, 0:1, :] = jnp.sum(r1[...] * r1[...], axis=0, keepdims=True)
+    norm0 = unpack(sums, 0)
+    curvature = unpack(sums, 1)
+    alpha = norm0 / curvature
+    r = b_ref[...] - alpha * w1[...]
+    sol_ref[...] = r
+    res_ref[...] = w1[...] - alpha * (
+        jnp.concatenate([inv[...], inv[...]], axis=1) * w1[...] + kernel_scale * sib[1, z]
+    )
+    pack(1, 0, r * r)
+    pack(1, 2, w1[...] * r)
+    for c in range(SUB):
+        for way in range(2):
+            wait(ring.at[1, way, 3, sub_rows(c)], r_recv.at[1, way, 3, c])
+    ar = res_ref[...] - (kernel_scale * alpha) * (ring[1, 0, 3] + ring[1, 1, 3])
+    res_ref[...] = ar
+    pack(1, 1, sol_ref[...] * ar)
     sum_start(1)
-    products(1)
     sum_middle(1)
-    ring_step(1, 2)
-    ring_step(1, 3)
-    norm1 = sum_finish(1)[0:1, :]
+    sums = sum_finish(1)
+    norm1 = unpack(sums, 0)
     beta = norm1 / norm0
-    for c in range(SUB):
-        rows = slice(c * SR, (c + 1) * SR)
-        w2[rows, :] = w1[rows, :] * inverse_radii[rows] + kernel_scale * ring_result(1, c)
-    direction = r1[...] + beta * b_ref[...]
-    w2[...] = (1.0 + beta) * w1[...] - alpha * w2[...]
-    ar_src[2] = jnp.zeros((8, R), F32)
-    ar_src[2, 0:1, :] = jnp.sum(direction * w2[...], axis=0, keepdims=True)
-    sum_start(2)
-    sum_middle(2)
-    step_size = norm1 / sum_finish(2)[0:1, :]
-    sol_ref[...] = alpha * b_ref[...] + step_size * (r1[...] + beta * b_ref[...])
-    res_ref[...] = r1[...] - step_size * w2[...]
-
-    wait(ar_plane.at[0, 0 : PLANE - 1], pos_send)
+    step_size = norm1 / (unpack(sums, 1) + 2.0 * beta * unpack(sums, 2) + beta * beta * curvature)
+    r = sol_ref[...]
+    sol_ref[...] = alpha * b_ref[...] + step_size * (r + beta * b_ref[...])
+    res_ref[...] = r - step_size * (res_ref[...] + beta * w1[...])
+
+    wait(gath.at[0, 0, 0 : B - 8], pos_send)
     for m in range(2):
         wait(gath.at[m, 0 : PLANE - 1], g_send.at[m])
         wait(gath.at[m, 0 : NZ - 1], r_send.at[m])
     wait(gath.at[1, 0:NZ], s_send.at[1])
-    for i in range(3):
+    for i in range(2):
         wait(ar_line.at[i, 0 : LINE - 1], ar_send.at[i, 1])
 
 
@@ -321,22 +364,22 @@
             pltpu.VMEM((PLANE, 8, B), F32),
             pltpu.VMEM((LINE, 8, B), F32),
             pltpu.VMEM((8, B), F32),
+            pltpu.VMEM((B, B), F32),
             pltpu.VMEM((B, R), F32),
-            pltpu.VMEM((B, R), F32),
-            pltpu.VMEM((B, R), F32),
-            pltpu.VMEM((3, 8, R), F32),
-            pltpu.VMEM((3, PLANE, 8, R), F32),
-            pltpu.VMEM((3, LINE, 8, R), F32),
+            pltpu.VMEM((2, 8, B), F32),
+            pltpu.VMEM((2, PLANE, 8, B), F32),
+            pltpu.VMEM((2, LINE, 8, B), F32),
             dma,
             dma((2,)),
             dma((2,)),
             dma((2, 2, PLANE)),
+            dma((2, 2, 2, NX)),
             dma((2,)),
             dma((2, NZ)),
             dma((2,)),
             dma((2, 2, 4, SUB)),
-            dma((3, 2)),
-            dma((3, 2)),
+            dma((2, 2)),
+            dma((2, 2)),
         ],
         compiler_params=pltpu.CompilerParams(
             collective_id=0, has_side_effects=True, vmem_limit_bytes=56 << 20

time: 109 us -> 98.4 us (0.903)
  Pallas kernels: 106 us -> 95.3 us
    pallas_call x1, Pallas kernels: 106 us -> 95.3 us  [body(): pl.pallas_call(functools.partial(kernel, kernel_scale, softening), out_sh...]
where the time goes in v2:
time: 98.4 us; the launch traced here: 98.2 us
  Pallas kernels  95.3 us (97%)
  local copies, waits for them, and re-layouts  2.26 us (2%)
    pallas_call x1, Pallas kernels, body(): pl.pallas_call(functools.partial(kernel, kernel_scale, softening), out_sh...  95.3 us
    unnamed x4, local copies, waits for them, and re-layouts  2.26 us

profile of v2, /device:TPU:1, one launch (start us, length us, event | category | flops | bytes accessed | tf_op | source)
XLA Modules:
  0.0 98.2 jit_solution(227469157510842895)
XLA Ops:
  0.6 95.3 %cg.1 = (f32[128,256]{1,0:T(8,128)}, f32[128,256]{1,0:T(8,128)}) custom-call(f32[3,128]{1,0:T(4,128)} %pos_ref.1, f32[1,128]{1,0:T(1,128)} %bitcast.1, f32[128,256]{1,0:T(8,128)} %b_ref.1), custom_call_target="tpu_custom_call" | custom-call | tf_op jit(solution)/shard_map/cg/pallas_call | solution.py:349
  96.0 0.0 copy-start
  96.0 1.6 %copy.7 = f32[128,256]{1,0:T(8,128)} copy(f32[128,256]{1,0:T(8,128)} %get-tuple-element.4) | data formatting | bytes 262144
  97.6 0.0 copy-done
  97.6 0.7 copy.8
Async XLA Ops:
  96.0 1.6 %copy-start = (f32[128,256]{1,0:T(8,128)S(1)}, f32[128,256]{1,0:T(8,128)}, u32[]{:S(2)}) copy-start(f32[128,256]{1,0:T(8,128)} %get-tuple-element.5) | copy-start | bytes 393220

commit v3 on v2

--- a/solution.py
+++ b/solution.py
@@ -29,8 +29,8 @@
 def kernel(
     kernel_scale, softening,
     pos_ref, rad_ref, b_ref, sol_ref, res_ref,
-    khi, klo, gath, vhi, vlo, part, sib, ring, xb, ppos, lpos, own_pos, inv, w1, ar_src, ar_plane, ar_line,
-    pos_send, pos_recv, g_send, g_recv, q_recv, s_send, s_recv, r_send, r_recv, ar_send, ar_recv,
+    khi, klo, gath, vhi, vlo, part, sib, ring, xb, ppos, lpos, own_pos, inv, w1, line, ar_src, ar_plane, ar_line,
+    pos_send, pos_recv, g_send, g_recv, q_recv, l_send, l_recv, s_send, s_recv, r_send, r_recv, ar_send, ar_recv,
 ):
     row, col = lax.axis_index("row"), lax.axis_index("col")
     x, y = col // 4, lax.rem(row, 4)
@@ -88,8 +88,10 @@
         return at_x(d) if h == 0 else at_y(d)
 
     def gather_start(m, src, h):
-        for d in (2, 1, 3):
+        for d in (1, 3, 2):
             send(src.at[half_rows(h)], gath.at[m, slot, half_rows(h)], g_send.at[m], g_recv.at[m, h, slot], first_peer(h, d))
+
+    def gather_second(m, src, h):
         for d in (1, 3):
             send(src.at[half_rows(h)], gath.at[m, slot, half_rows(h)], g_send.at[m], g_recv.at[m, h, slot], second_peer(h, d))
 
@@ -119,6 +121,24 @@
             for h in range(2):
                 for q in range(2):
                     wait(quarter(m, h, plane_slot(h, o, 2), q), q_recv.at[m, h, q, first_at(h, o)])
+
+    def line_step(m, j):
+        for p in range(2):
+            for way in range(2):
+                if j == 4 and p != way:
+                    continue
+                source = at_z(1 - j + NZ if way == 0 else j - 1)
+                piece = line.at[m, source, half_rows(p)]
+                if j > 1:
+                    wait(piece, l_recv.at[m, source, p])
+                peer = device(x, y, at_z(1 if way == 0 else NZ - 1), k)
+                send(piece, piece, l_send.at[m], l_recv.at[m, source, p], peer)
+
+    def line_finish(m):
+        wait(line.at[m, at_z(5), half_rows(1)], l_recv.at[m, at_z(5), 1])
+        wait(line.at[m, at_z(3), half_rows(0)], l_recv.at[m, at_z(3), 0])
+        for p in range(2):
+            wait(line.at[m, at_z(4), half_rows(p)], l_recv.at[m, at_z(4), p])
 
     def pack(i, j, term):
         column = jnp.sum(term, axis=0, keepdims=True)
@@ -155,8 +175,12 @@
         send(own_pos, lpos.at[line_slot], pos_send, pos_recv.at[1], peer)
     for peer in plane_peers:
         send(own_pos, ppos.at[slot], pos_send, pos_recv.at[0], peer)
-    gather_start(0, b_ref, 0)
-    gather_start(0, b_ref, 1)
+    for h in range(2):
+        gather_start(0, b_ref, h)
+    for h in range(2):
+        gather_second(0, b_ref, h)
+    line[0, z] = b_ref[...]
+    line_step(0, 1)
     ppos[slot] = own_pos[...]
     lpos[line_slot] = own_pos[...]
     gath[0, slot] = b_ref[...]
@@ -189,8 +213,10 @@
 
     lax.fori_loop(0, 6, evaluate, 0)
     gather_forward(0, (1, 3))
+    line_step(0, 2)
     lax.fori_loop(6, 12, evaluate, 0)
     gather_forward(0, (2,))
+    line_step(0, 3)
     lax.fori_loop(12, LINE, evaluate, 0)
 
     def split_values(m):
@@ -219,20 +245,13 @@
         sib[m, dest] = sib[m, dest] + part[mine, :]
 
     def ring_step(m, s):
-        if s == 0:
-            for c in range(SUB // 2):
-                for way in range(2):
-                    cc = c if way == 0 else c + SUB // 2
-                    piece = sib.at[m, ring_target(way, 0), sub_rows(cc)]
-                    send(piece, ring.at[m, way, 0, sub_rows(cc)], r_send.at[m], r_recv.at[m, way, 0, cc], ring_peer(way))
-            return
-        late = ((0, 1), (2, 3))
         for i in range(SUB):
             for way in range(2):
-                order = late[1 - way] + late[way]
-                c = order[i]
+                c = 2 * (i % (SUB // 2)) + (1 - way if i < SUB // 2 else way)
+                if s == 0 and c % 2 != way:
+                    continue
                 dest = ring_target(way, s)
-                if s == 1 and c not in late[way]:
+                if s == 0 or (s == 1 and c % 2 != way):
                     piece = sib.at[m, dest, sub_rows(c)]
                 else:
                     piece = ring.at[m, way, s - 1, sub_rows(c)]
@@ -271,20 +290,21 @@
             join_sibling(m, at_z(5))
             ring_step(m, 1)
 
-        hooks = ((1, first), (4, second))
+        hooks = ((1, first), (4 if m == 0 else 6, second))
         lax.fori_loop(0, NZ, step, 0)
         for d in (2, 6):
             join_sibling(m, at_z(d))
-        ring_step(m, 2)
-        for d in (1, 7):
+        if m == 0:
+            ring_step(m, 2)
+        for d in (1, 7, 0):
             join_sibling(m, at_z(d))
-        ring_step(m, 3)
-        join_sibling(m, z)
 
     ar_src[...] = jnp.zeros_like(ar_src)
+    line_step(0, 4)
     gather_finish(0)
     split_values(0)
     products(0)
+    ring_step(0, 3)
     pack(0, 0, b_ref[...] * b_ref[...])
     for h in range(2):
         for c in range(h * SUB // 2, (h + 1) * SUB // 2):
@@ -292,36 +312,50 @@
             own = jnp.concatenate([inv[rows, :], inv[rows, :]], axis=1) * b_ref[rows, :]
             w1[rows, :] = own + kernel_scale * ring_result(0, c)
         gather_start(1, w1, h)
+    for h in range(2):
+        gather_second(1, w1, h)
+    line[1, z] = w1[...]
+    line_step(1, 1)
     gath[1, slot] = w1[...]
     pack(0, 1, b_ref[...] * w1[...])
-    sum_start(0)
     wait(gath.at[0, 0:NZ], s_send.at[0])
     gather_spread(1)
+    line_step(1, 2)
+    sum_start(0)
     gather_forward(1, (0, 1, 3))
-    sum_middle(0)
+    line_step(1, 3)
     gather_forward(1, (2,))
     gather_finish(1)
+    sum_middle(0)
+    line_step(1, 4)
     split_values(1)
+    line_finish(0)
     products(1)
     sums = sum_finish(0)
     norm0 = unpack(sums, 0)
     curvature = unpack(sums, 1)
     alpha = norm0 / curvature
+    line_finish(1)
     r = b_ref[...] - alpha * w1[...]
     sol_ref[...] = r
-    res_ref[...] = w1[...] - alpha * (
-        jnp.concatenate([inv[...], inv[...]], axis=1) * w1[...] + kernel_scale * sib[1, z]
-    )
+    scaled = jnp.concatenate([inv[...], inv[...]], axis=1) * w1[...]
+
+    def meet(dest, total):
+        return total + (line[0, dest] - alpha * line[1, dest]) * sib[1, dest]
+
+    met = lax.fori_loop(0, NZ, meet, jnp.zeros((B, R), F32))
     pack(1, 0, r * r)
+    pack(1, 1, r * (w1[...] - alpha * scaled) - (kernel_scale * alpha) * met)
     pack(1, 2, w1[...] * r)
+    sum_start(1)
+    ring_step(1, 2)
+    sum_middle(1)
+    ring_step(1, 3)
+    res_ref[...] = w1[...] - alpha * (scaled + kernel_scale * sib[1, z])
     for c in range(SUB):
         for way in range(2):
             wait(ring.at[1, way, 3, sub_rows(c)], r_recv.at[1, way, 3, c])
-    ar = res_ref[...] - (kernel_scale * alpha) * (ring[1, 0, 3] + ring[1, 1, 3])
-    res_ref[...] = ar
-    pack(1, 1, sol_ref[...] * ar)
-    sum_start(1)
-    sum_middle(1)
+    res_ref[...] = res_ref[...] - (kernel_scale * alpha) * (ring[1, 0, 3] + ring[1, 1, 3])
     sums = sum_finish(1)
     norm1 = unpack(sums, 0)
     beta = norm1 / norm0
@@ -334,6 +368,7 @@
     for m in range(2):
         wait(gath.at[m, 0 : PLANE - 1], g_send.at[m])
         wait(gath.at[m, 0 : NZ - 1], r_send.at[m])
+        wait(gath.at[m, 0 : NZ - 1], l_send.at[m])
     wait(gath.at[1, 0:NZ], s_send.at[1])
     for i in range(2):
         wait(ar_line.at[i, 0 : LINE - 1], ar_send.at[i, 1])
@@ -366,6 +401,7 @@
             pltpu.VMEM((8, B), F32),
             pltpu.VMEM((B, B), F32),
             pltpu.VMEM((B, R), F32),
+            pltpu.VMEM((2, NZ, B, R), F32),
             pltpu.VMEM((2, 8, B), F32),
             pltpu.VMEM((2, PLANE, 8, B), F32),
             pltpu.VMEM((2, LINE, 8, B), F32),
@@ -374,6 +410,8 @@
             dma((2,)),
             dma((2, 2, PLANE)),
             dma((2, 2, 2, NX)),
+            dma((2,)),
+            dma((2, NZ, 2)),
             dma((2,)),
             dma((2, NZ)),
             dma((2,)),

time: 98.4 us -> 92.7 us (0.942)
  Pallas kernels: 95.3 us -> 89.7 us
    pallas_call x1, Pallas kernels: 95.3 us -> 89.7 us  [body(): pl.pallas_call(functools.partial(kernel, kernel_scale, softening), out_sh...]
where the time goes in v3:
time: 92.7 us; the launch traced here: 92.6 us
  Pallas kernels  89.7 us (97%)
  local copies, waits for them, and re-layouts  2.26 us (2%)
    pallas_call x1, Pallas kernels, body(): pl.pallas_call(functools.partial(kernel, kernel_scale, softening), out_sh...  89.7 us
    unnamed x4, local copies, waits for them, and re-layouts  2.26 us

profile of v3, /device:TPU:1, one launch (start us, length us, event | category | flops | bytes accessed | tf_op | source)
XLA Modules:
  0.0 92.6 jit_solution(10160599220253611443)
XLA Ops:
  0.6 89.7 %cg.1 = (f32[128,256]{1,0:T(8,128)}, f32[128,256]{1,0:T(8,128)}) custom-call(f32[3,128]{1,0:T(4,128)} %pos_ref.1, f32[1,128]{1,0:T(1,128)} %bitcast.1, f32[128,256]{1,0:T(8,128)} %b_ref.1), custom_call_target="tpu_custom_call" | custom-call | tf_op jit(solution)/shard_map/cg/pallas_call | solution.py:384
  90.3 0.0 copy-start
  90.3 1.6 %copy.7 = f32[128,256]{1,0:T(8,128)} copy(f32[128,256]{1,0:T(8,128)} %get-tuple-element.4) | data formatting | bytes 262144
  92.0 0.0 copy-done
  92.0 0.7 copy.8
Async XLA Ops:
  90.3 1.6 %copy-start = (f32[128,256]{1,0:T(8,128)S(1)}, f32[128,256]{1,0:T(8,128)}, u32[]{:S(2)}) copy-start(f32[128,256]{1,0:T(8,128)} %get-tuple-element.5) | copy-start | bytes 393220

commit v4 on v3

--- a/solution.py
+++ b/solution.py
@@ -216,7 +216,6 @@
     line_step(0, 2)
     lax.fori_loop(6, 12, evaluate, 0)
     gather_forward(0, (2,))
-    line_step(0, 3)
     lax.fori_loop(12, LINE, evaluate, 0)
 
     def split_values(m):
@@ -290,7 +289,7 @@
             join_sibling(m, at_z(5))
             ring_step(m, 1)
 
-        hooks = ((1, first), (4 if m == 0 else 6, second))
+        hooks = ((1, first), (4, second)) if m == 0 else ((0, lambda: line_step(1, 4)), (1, first), (6, second))
         lax.fori_loop(0, NZ, step, 0)
         for d in (2, 6):
             join_sibling(m, at_z(d))
@@ -300,9 +299,9 @@
             join_sibling(m, at_z(d))
 
     ar_src[...] = jnp.zeros_like(ar_src)
-    line_step(0, 4)
     gather_finish(0)
     split_values(0)
+    line_step(0, 3)
     products(0)
     ring_step(0, 3)
     pack(0, 0, b_ref[...] * b_ref[...])
@@ -320,6 +319,7 @@
     pack(0, 1, b_ref[...] * w1[...])
     wait(gath.at[0, 0:NZ], s_send.at[0])
     gather_spread(1)
+    line_step(0, 4)
     line_step(1, 2)
     sum_start(0)
     gather_forward(1, (0, 1, 3))
@@ -327,14 +327,13 @@
     gather_forward(1, (2,))
     gather_finish(1)
     sum_middle(0)
-    line_step(1, 4)
     split_values(1)
-    line_finish(0)
     products(1)
     sums = sum_finish(0)
     norm0 = unpack(sums, 0)
     curvature = unpack(sums, 1)
     alpha = norm0 / curvature
+    line_finish(0)
     line_finish(1)
     r = b_ref[...] - alpha * w1[...]
     sol_ref[...] = r

time: 92.7 us -> 90.6 us (0.977)
  Pallas kernels: 89.7 us -> 87.6 us
    pallas_call x1, Pallas kernels: 89.7 us -> 87.6 us  [body(): pl.pallas_call(functools.partial(kernel, kernel_scale, softening), out_sh...]
where the time goes in v4:
time: 90.6 us; the launch traced here: 90.5 us
  Pallas kernels  87.6 us (97%)
  local copies, waits for them, and re-layouts  2.26 us (2%)
    pallas_call x1, Pallas kernels, body(): pl.pallas_call(functools.partial(kernel, kernel_scale, softening), out_sh...  87.6 us
    unnamed x4, local copies, waits for them, and re-layouts  2.26 us

profile of v4, /device:TPU:1, one launch (start us, length us, event | category | flops | bytes accessed | tf_op | source)
XLA Modules:
  0.0 90.5 jit_solution(17021349757762010595)
XLA Ops:
  0.6 87.6 %cg.1 = (f32[128,256]{1,0:T(8,128)}, f32[128,256]{1,0:T(8,128)}) custom-call(f32[3,128]{1,0:T(4,128)} %pos_ref.1, f32[1,128]{1,0:T(1,128)} %bitcast.1, f32[128,256]{1,0:T(8,128)} %b_ref.1), custom_call_target="tpu_custom_call" | custom-call | tf_op jit(solution)/shard_map/cg/pallas_call | solution.py:383
  88.2 0.0 copy-start
  88.2 1.6 %copy.7 = f32[128,256]{1,0:T(8,128)} copy(f32[128,256]{1,0:T(8,128)} %get-tuple-element.4) | data formatting | bytes 262144
  89.8 0.0 copy-done
  89.8 0.7 copy.8
Async XLA Ops:
  88.2 1.6 %copy-start = (f32[128,256]{1,0:T(8,128)S(1)}, f32[128,256]{1,0:T(8,128)}, u32[]{:S(2)}) copy-start(f32[128,256]{1,0:T(8,128)} %get-tuple-element.5) | copy-start | bytes 393220

commit v5 on v4

--- a/solution.py
+++ b/solution.py
@@ -289,7 +289,7 @@
             join_sibling(m, at_z(5))
             ring_step(m, 1)
 
-        hooks = ((1, first), (4, second)) if m == 0 else ((0, lambda: line_step(1, 4)), (1, first), (6, second))
+        hooks = ((1, first), (4, second)) if m == 0 else ((1, first), (3, lambda: line_step(1, 4)), (6, second))
         lax.fori_loop(0, NZ, step, 0)
         for d in (2, 6):
             join_sibling(m, at_z(d))
@@ -323,10 +323,10 @@
     line_step(1, 2)
     sum_start(0)
     gather_forward(1, (0, 1, 3))
+    gather_forward(1, (2,))
+    sum_middle(0)
+    gather_finish(1)
     line_step(1, 3)
-    gather_forward(1, (2,))
-    gather_finish(1)
-    sum_middle(0)
     split_values(1)
     products(1)
     sums = sum_finish(0)

time: 90.6 us -> 89.2 us (0.985)
  Pallas kernels: 87.6 us -> 86.2 us
    pallas_call x1, Pallas kernels: 87.6 us -> 86.2 us  [body(): pl.pallas_call(functools.partial(kernel, kernel_scale, softening), out_sh...]
where the time goes in v5:
time: 89.2 us; the launch traced here: 89.1 us
  Pallas kernels  86.2 us (97%)
  local copies, waits for them, and re-layouts  2.26 us (3%)
    pallas_call x1, Pallas kernels, body(): pl.pallas_call(functools.partial(kernel, kernel_scale, softening), out_sh...  86.2 us
    unnamed x4, local copies, waits for them, and re-layouts  2.26 us

profile of v5, /device:TPU:1, one launch (start us, length us, event | category | flops | bytes accessed | tf_op | source)
XLA Modules:
  0.0 89.1 jit_solution(14634836601850042361)
XLA Ops:
  0.6 86.2 %cg.1 = (f32[128,256]{1,0:T(8,128)}, f32[128,256]{1,0:T(8,128)}) custom-call(f32[3,128]{1,0:T(4,128)} %pos_ref.1, f32[1,128]{1,0:T(1,128)} %bitcast.1, f32[128,256]{1,0:T(8,128)} %b_ref.1), custom_call_target="tpu_custom_call" | custom-call | tf_op jit(solution)/shard_map/cg/pallas_call | solution.py:383
  86.8 0.0 copy-start
  86.8 1.6 %copy.7 = f32[128,256]{1,0:T(8,128)} copy(f32[128,256]{1,0:T(8,128)} %get-tuple-element.4) | data formatting | bytes 262144
  88.4 0.0 copy-done
  88.5 0.7 copy.8
Async XLA Ops:
  86.8 1.6 %copy-start = (f32[128,256]{1,0:T(8,128)S(1)}, f32[128,256]{1,0:T(8,128)}, u32[]{:S(2)}) copy-start(f32[128,256]{1,0:T(8,128)} %get-tuple-element.5) | copy-start | bytes 393220
